TPU v7x, 256 devices: a whole 4x4x8 slice. The times are simulated.
256 devices in a mesh: section: 8 (over y, core), dp: 32 (over z, x).
Axes of the slice: x: 4, y: 4, z: 8, core: 2. Of those that a mesh axis runs over, the one named last changes fastest.
Arguments:
- hidden_in: bfloat16 [4, 1024, 8192], P(None, 'dp'), may hold values from -6 to 6
- cotangent: bfloat16 [4, 1024, 8192], P(None, 'dp'), may hold values from -6 to 6
- adapter_in: bfloat16 [8, 8192, 128], P('section', 'dp'), may hold values from -0.0625 to 0.0625
- adapter_out: bfloat16 [8, 128, 8192], P('section', None, 'dp'), may hold values from -0.5 to 0.5
- norm_gain: bfloat16 [8, 8192], P('section', 'dp'), may hold values from 0.5 to 1.5
- user_of_row: int32 [4, 1024], P(None, 'dp'), may hold values from 0 to 63, as said below
- included: int32 [4, 64], P(None, 'dp'), may hold values 0 or 1
Outputs:
- grad_in: float32 [8, 8192, 128], P('section', 'dp')
- grad_out: float32 [8, 128, 8192], P('section', None, 'dp')
- user_weights: float32 [4, 64], P(None, 'dp')
Inputs may be any that keep to these rules, and one draw needn't show every extreme that they name: `user_of_row`: within one micro-batch, the rows of the j-th block of 32 rows belong to users j * 2 to j * 2 + 1, in rising order, each of them with one row or more.
All inputs are finite; a program needn't handle non-finite values. No bound on the sum of `included` on one device may be relied on, other than what follows from the above.
Results may differ from a plain program's by a relative error of at most 0.018.
Values may be sent and summed in bfloat16 or wider, within the bound.
A program may use at most 64 MiB of HBM per device.

v0:
```python
import math
import jax
import jax.numpy as jnp
from jax import lax
from jax.sharding import Mesh
from jax.sharding import PartitionSpec as P

DP = ("dp_0", "dp_1")


def gather_turned(arrays, axis, dims):
    turned = [jnp.moveaxis(a, dim, 0) for a, dim in zip(arrays, dims)]
    both = jnp.concatenate([t.reshape(len(t), -1) for t in turned], axis=1)
    result, at, done = (lax.all_gather(both, axis, axis=0, tiled=True), 0, [])
    for t, dim in zip(turned, dims):
        section = result[:, at : at + t[0].size].reshape(-1, *t.shape[1:])
        done.append(jnp.moveaxis(section, 0, dim))
        at += t[0].size
    return tuple(done)


def from_behind(block, axis, distance):
    devices = range(lax.axis_size(axis))
    route = [(i - distance, i) for i in devices if i - distance in devices]
    return lax.ppermute(block, axis, route)


def copy_for_each(x, axis):
    copies = jnp.broadcast_to(x, (lax.axis_size(axis), *x.shape))
    return lax.all_to_all(copies, axis, split_axis=0, concat_axis=0, tiled=True)


def taken_together(x, axis):
    return copy_for_each(x, axis).sum(axis=0)


def summed_rows(terms, axes):
    running = terms.astype(jnp.bfloat16)
    for axis in axes:
        running = lax.psum_scatter(running, axis, scatter_dimension=0, tiled=True)
    return running.astype(jnp.float32)


def normalize(stream_in, gain):
    stream = stream_in.astype(jnp.float32)
    scale = lax.rsqrt(jnp.mean(stream * stream, -1, keepdims=True) + 1e-05)
    unit = stream * scale
    normed = (unit * gain).astype(jnp.bfloat16)
    return (stream, scale, unit, normed)


def place(store, value, index, active):
    old = lax.dynamic_index_in_dim(store, index, 0, keepdims=False)
    return lax.dynamic_update_index_in_dim(store, jnp.where(active, value, old), index, 0)


def contract_last(left, right):
    return lax.dot_general(
        left, right, (((1,), (1,)), ((), ())), preferred_element_type=jnp.float32
    )


def contract_first(left, right):
    return lax.dot_general(
        left, right, (((0,), (0,)), ((), ())), preferred_element_type=jnp.float32
    )


def ghost(normed, err, low, delta, owners, onehot):
    same = owners[:, None] == owners[None, :]
    pairs = contract_last(normed, normed) * contract_last(err, err) + contract_last(
        low, low
    ) * contract_last(delta, delta)
    pairs = jnp.where(same, pairs, jnp.zeros_like(pairs))
    return jnp.sum(onehot * jnp.sum(pairs, -1)[:, None], 0)


def shards(hidden_in, cotangent, adapter_in, adapter_out, norm_gain, user_of_row, included):
    sections = lax.axis_size("section")
    section = lax.axis_index("section")
    dp_index = lax.axis_index(DP)
    a_full, b_full, g_full = gather_turned((adapter_in, adapter_out, norm_gain), DP, (1, 2, 1))
    a_mat = a_full[0]
    b_mat = b_full[0]
    gain = g_full[0].astype(jnp.float32)
    micro, rows, width = hidden_in.shape
    rank = a_mat.shape[1]
    users = included.shape[1]
    ticks = micro + sections - 1
    local_ids = user_of_row - dp_index * users
    onehot = (local_ids[:, :, None] == jnp.arange(users, dtype=jnp.int32)[None, None, :]).astype(
        jnp.float32
    )

    def forward_tick(carry, tick):
        incoming, keep_h, keep_n, keep_z = carry
        slot = tick - section
        active = (slot >= 0) & (slot < micro)
        index = jnp.clip(slot, 0, micro - 1)
        source = lax.dynamic_index_in_dim(hidden_in, index, 0, keepdims=False)
        current = jnp.where(section == 0, source, incoming)
        stream, scale, unit, normed = normalize(current, gain)
        low = jnp.dot(normed, a_mat, preferred_element_type=jnp.float32).astype(jnp.bfloat16)
        result = (stream + jnp.dot(low, b_mat, preferred_element_type=jnp.float32)).astype(
            jnp.bfloat16
        )
        keep_h = place(keep_h, current, index, active)
        keep_n = place(keep_n, normed, index, active)
        keep_z = place(keep_z, low, index, active)
        outgoing = from_behind(result, "section", 1)
        return ((outgoing, keep_h, keep_n, keep_z), None)

    start_fwd = (
        jnp.zeros((rows, width), jnp.bfloat16),
        jnp.zeros_like(hidden_in),
        jnp.zeros_like(hidden_in),
        jnp.zeros((micro, rows, rank), jnp.bfloat16),
    )
    (unused, keep_h, keep_n, keep_z), unused_out = lax.scan(
        forward_tick, start_fwd, jnp.arange(ticks, dtype=jnp.int32)
    )

    def backward_tick(carry, tick):
        incoming, carried, keep_e, keep_d, keep_p = carry
        slot = tick - (sections - 1 - section)
        active = (slot >= 0) & (slot < micro)
        index = jnp.clip(slot, 0, micro - 1)
        source = lax.dynamic_index_in_dim(cotangent, index, 0, keepdims=False)
        delta = jnp.where(section == sections - 1, source, incoming)
        current = lax.dynamic_index_in_dim(keep_h, index, 0, keepdims=False)
        normed = lax.dynamic_index_in_dim(keep_n, index, 0, keepdims=False)
        low = lax.dynamic_index_in_dim(keep_z, index, 0, keepdims=False)
        owners = lax.dynamic_index_in_dim(user_of_row, index, 0, keepdims=False)
        hot = lax.dynamic_index_in_dim(onehot, index, 0, keepdims=False)
        stream, scale, unit, unused_n = normalize(current, gain)
        err = contract_last(delta, b_mat).astype(jnp.bfloat16)
        slope = contract_last(err, a_mat) * gain
        grad_h = scale * (slope - unit * jnp.mean(slope * unit, -1, keepdims=True))
        previous = (delta.astype(jnp.float32) + grad_h).astype(jnp.bfloat16)
        partial_value = ghost(normed, err, low, delta, owners, hot)
        keep_e = place(keep_e, err, index, active)
        keep_d = place(keep_d, delta, index, active)
        keep_p = place(keep_p, partial_value, index, active)
        outgoing = from_behind(previous, "section", -1)
        return ((outgoing, carried, keep_e, keep_d, keep_p), None)

    start_bwd = (
        jnp.zeros((rows, width), jnp.bfloat16),
        jnp.zeros((users,), jnp.float32),
        jnp.zeros((micro, rows, rank), jnp.bfloat16),
        jnp.zeros_like(cotangent),
        jnp.zeros((micro, users), jnp.float32),
    )
    (unused_a, unused_b, keep_e, keep_d, keep_p), unused_out = lax.scan(
        backward_tick, start_bwd, jnp.arange(ticks, dtype=jnp.int32)
    )
    total = taken_together(keep_p, "section")
    bound = 0.8 * math.sqrt(sections * (rows // users) * width * width)
    user_weights = included.astype(jnp.float32) * (bound / jnp.maximum(jnp.sqrt(total), bound))
    row_weight = jnp.sum(onehot * user_weights[:, None, :], -1)[:, :, None]
    weighted_err = (
        (row_weight * keep_e.astype(jnp.float32)).astype(jnp.bfloat16).reshape(micro * rows, rank)
    )
    weighted_delta = (
        (row_weight * keep_d.astype(jnp.float32)).astype(jnp.bfloat16).reshape(micro * rows, width)
    )
    normed_rows = keep_n.reshape(micro * rows, width)
    low_rows = keep_z.reshape(micro * rows, rank)
    shard = summed_rows(
        jnp.concatenate(
            [contract_first(normed_rows, weighted_err), contract_first(weighted_delta, low_rows)], 1
        ),
        DP,
    )
    grad_in = shard[:, :rank]
    grad_out = shard[:, rank:].T
    return (grad_in[None], grad_out[None], user_weights)


def solution(mesh):
    torus = Mesh(mesh.devices.reshape(mesh.shape["section"], 8, 4), ("section", "dp_0", "dp_1"))
    return jax.shard_map(
        shards,
        mesh=torus,
        in_specs=(
            P(None, DP, None),
            P(None, DP, None),
            P("section", DP, None),
            P("section", None, DP),
            P("section", DP),
            P(None, DP),
            P(None, DP),
        ),
        out_specs=(P("section", DP, None), P("section", None, DP), P(None, DP)),
        check_vma=False,
    )
```

profile of v0, /device:TPU:8, one launch (start us, length us, event | category | flops | bytes accessed | tf_op | source)
XLA Modules:
  0.0 595.3 jit_solution(11264606444383854326)
XLA Ops:
  10.5 85.9 %all-gather.2.cloned.1.call-done = bf16[8192,257]{0,1:T(8,128)(2,1)} async-done(((bf16[256,257]{0,1:T(8,128)(2,1)}), bf16[8192,257]{0,1:T(8,128)(2,1)}) %all-gather.2.cloned.1.call-update) | async-done | bytes 4210704 | tf_op jit(solution)/shard_map/all_gather | solution.py:14
  96.3 3.9 slice_bitcast_fusion
  100.3 4.1 copy.19
  108.4 178.3 %while.35 = (s32[]{:T(128)}, bf16[32,8192]{1,0:T(8,128)(2,1)S(1)}, bf16[4,32,8192]{2,1,0:T(8,128)(2,1)}, bf16[4,32,8192]{2,1,0:T(8,128)(2,1)}, bf16[4,32,128]{2,...) while((s32[]{:T(128)}, bf16[32,8192]{1,0:T(8,128)(2,1)S(1)}, ...), condition=%wide.region_2.3_spmd, body=%wide.region_0.2_spmd.sunk | while | flops 138682400 | bytes 23185208 | solution.py:119
  118.2 6.4 %collective-permute-done = bf16[32,8192]{1,0:T(8,128)(2,1)S(1)} collective-permute-done((bf16[32,8192]{1,0:T(8,128)(2,1)S(1)}, bf16[32,8192]{1,0:T(8,128)(2,1)S(1)}, u32[]{:S(2)}, u32[]{:S(2)}) %collective-permute-start) | collective-permute-done | bytes 524320 | tf_op jit(solution)/shard_map/while/body/eval_jaxpr/ppermute | solution.py:25
  134.4 6.4 %collective-permute-done = bf16[32,8192]{1,0:T(8,128)(2,1)S(1)} collective-permute-done((bf16[32,8192]{1,0:T(8,128)(2,1)S(1)}, bf16[32,8192]{1,0:T(8,128)(2,1)S(1)}, u32[]{:S(2)}, u32[]{:S(2)}) %collective-permute-start) | collective-permute-done | bytes 524320 | tf_op jit(solution)/shard_map/while/body/eval_jaxpr/ppermute | solution.py:25
  150.6 6.4 %collective-permute-done = bf16[32,8192]{1,0:T(8,128)(2,1)S(1)} collective-permute-done((bf16[32,8192]{1,0:T(8,128)(2,1)S(1)}, bf16[32,8192]{1,0:T(8,128)(2,1)S(1)}, u32[]{:S(2)}, u32[]{:S(2)}) %collective-permute-start) | collective-permute-done | bytes 524320 | tf_op jit(solution)/shard_map/while/body/eval_jaxpr/ppermute | solution.py:25
  166.8 6.4 %collective-permute-done = bf16[32,8192]{1,0:T(8,128)(2,1)S(1)} collective-permute-done((bf16[32,8192]{1,0:T(8,128)(2,1)S(1)}, bf16[32,8192]{1,0:T(8,128)(2,1)S(1)}, u32[]{:S(2)}, u32[]{:S(2)}) %collective-permute-start) | collective-permute-done | bytes 524320 | tf_op jit(solution)/shard_map/while/body/eval_jaxpr/ppermute | solution.py:25
  183.0 6.4 %collective-permute-done = bf16[32,8192]{1,0:T(8,128)(2,1)S(1)} collective-permute-done((bf16[32,8192]{1,0:T(8,128)(2,1)S(1)}, bf16[32,8192]{1,0:T(8,128)(2,1)S(1)}, u32[]{:S(2)}, u32[]{:S(2)}) %collective-permute-start) | collective-permute-done | bytes 524320 | tf_op jit(solution)/shard_map/while/body/eval_jaxpr/ppermute | solution.py:25
  199.2 6.4 %collective-permute-done = bf16[32,8192]{1,0:T(8,128)(2,1)S(1)} collective-permute-done((bf16[32,8192]{1,0:T(8,128)(2,1)S(1)}, bf16[32,8192]{1,0:T(8,128)(2,1)S(1)}, u32[]{:S(2)}, u32[]{:S(2)}) %collective-permute-start) | collective-permute-done | bytes 524320 | tf_op jit(solution)/shard_map/while/body/eval_jaxpr/ppermute | solution.py:25
  215.5 6.4 %collective-permute-done = bf16[32,8192]{1,0:T(8,128)(2,1)S(1)} collective-permute-done((bf16[32,8192]{1,0:T(8,128)(2,1)S(1)}, bf16[32,8192]{1,0:T(8,128)(2,1)S(1)}, u32[]{:S(2)}, u32[]{:S(2)}) %collective-permute-start) | collective-permute-done | bytes 524320 | tf_op jit(solution)/shard_map/while/body/eval_jaxpr/ppermute | solution.py:25
  231.7 6.4 %collective-permute-done = bf16[32,8192]{1,0:T(8,128)(2,1)S(1)} collective-permute-done((bf16[32,8192]{1,0:T(8,128)(2,1)S(1)}, bf16[32,8192]{1,0:T(8,128)(2,1)S(1)}, u32[]{:S(2)}, u32[]{:S(2)}) %collective-permute-start) | collective-permute-done | bytes 524320 | tf_op jit(solution)/shard_map/while/body/eval_jaxpr/ppermute | solution.py:25
  247.9 6.4 %collective-permute-done = bf16[32,8192]{1,0:T(8,128)(2,1)S(1)} collective-permute-done((bf16[32,8192]{1,0:T(8,128)(2,1)S(1)}, bf16[32,8192]{1,0:T(8,128)(2,1)S(1)}, u32[]{:S(2)}, u32[]{:S(2)}) %collective-permute-start) | collective-permute-done | bytes 524320 | tf_op jit(solution)/shard_map/while/body/eval_jaxpr/ppermute | solution.py:25
  264.1 6.4 %collective-permute-done = bf16[32,8192]{1,0:T(8,128)(2,1)S(1)} collective-permute-done((bf16[32,8192]{1,0:T(8,128)(2,1)S(1)}, bf16[32,8192]{1,0:T(8,128)(2,1)S(1)}, u32[]{:S(2)}, u32[]{:S(2)}) %collective-permute-start) | collective-permute-done | bytes 524320 | tf_op jit(solution)/shard_map/while/body/eval_jaxpr/ppermute | solution.py:25
  280.3 6.4 %collective-permute-done = bf16[32,8192]{1,0:T(8,128)(2,1)S(1)} collective-permute-done((bf16[32,8192]{1,0:T(8,128)(2,1)S(1)}, bf16[32,8192]{1,0:T(8,128)(2,1)S(1)}, u32[]{:S(2)}, u32[]{:S(2)}) %collective-permute-start) | collective-permute-done | bytes 524320 | tf_op jit(solution)/shard_map/while/body/eval_jaxpr/ppermute | solution.py:25
  288.4 201.6 %while.36 = (s32[]{:T(128)}, bf16[32,8192]{1,0:T(8,128)(2,1)S(1)}, bf16[4,32,128]{2,1,0:T(8,128)(2,1)S(1)}, bf16[4,32,8192]{2,1,0:T(8,128)(2,1)}, f32[4,2]{1,0:T...) while((s32[]{:T(128)}, bf16[32,8192]{1,0:T(8,128)(2,1)S(1)}, ...), condition=%wide.region_8.9_spmd, body=%wide.region_3.8_spmd.sunk | while | flops 173029504 | bytes 33156040 | solution.py:154
  313.0 3.8 collective-permute-start.1
  319.7 3.8 collective-permute-done.1
  331.5 3.8 collective-permute-start.1
  350.0 3.8 collective-permute-start.1
  368.5 3.8 collective-permute-start.1
  375.2 3.8 collective-permute-done.1
  387.0 3.8 collective-permute-start.1
  405.5 3.8 collective-permute-start.1
  424.0 3.8 collective-permute-start.1
  461.0 3.8 collective-permute-start.1
  467.7 3.8 collective-permute-done.1
  479.5 3.8 collective-permute-start.1
  486.2 3.8 collective-permute-done.1
  490.1 9.5 %all_to_all.5 = f32[8,4,2]{1,2,0:T(2,128)S(1)} all-to-all(f32[8,4,2]{1,2,0:T(2,128)S(1)} %broadcast_in_dim.47), channel_id=1, replica_groups=mesh['section'=8,'dp_0'=8,'dp_1'=4] {'section'}, dimensions={0} | all-to-all | bytes 512 | tf_op jit(solution)/shard_map/all_to_all | solution.py:30
  505.7 55.4 %reduce-scatter.3.cloned.1.call-done = bf16[1024,256]{0,1:T(8,128)(2,1)} async-done(((bf16[8192,256]{0,1:T(8,128)(2,1)}), bf16[1024,256]{0,1:T(8,128)(2,1)}) %reduce-scatter.3.cloned.1.call-update) | async-done | bytes 524304 | tf_op jit(solution)/shard_map/reduce_scatter | solution.py:40
  561.1 25.3 %reduce-scatter.5.cloned.1.call-done = bf16[256,256]{0,1:T(8,128)(2,1)} async-done(((bf16[1024,256]{0,1:T(8,128)(2,1)}), bf16[256,256]{0,1:T(8,128)(2,1)}) %reduce-scatter.5.cloned.1.call-update) | async-done | bytes 131088 | tf_op jit(solution)/shard_map/reduce_scatter | solution.py:40
  (433 shorter events, 261.4 us)
Async XLA Ops:
  7.2 89.2 %all-gather.2.cloned.1.call-start = ((), (), s32[]{:S(2)}) async-start(), calls=%async_computation.3 | async-start | bytes 4460544 | tf_op jit(solution)/shard_map/all_gather | solution.py:14
  9.7 551.3 %reduce-scatter.3.cloned.1.call-start = ((), (), s32[]{:S(2)}) async-start(), calls=%async_computation.4 | async-start | bytes 4718592 | tf_op jit(solution)/shard_map/reduce_scatter | solution.py:40
  114.1 10.5 %collective-permute-start = (bf16[32,8192]{1,0:T(8,128)(2,1)S(1)}, bf16[32,8192]{1,0:T(8,128)(2,1)S(1)}, u32[]{:S(2)}, u32[]{:S(2)}) collective-permute-start(bf16[32,8192]{1,0:T(8,128)(2,1)S(1)} %fusion.73), channel_id=1, source_target_pairs={{0,32},{32,64},{64,96},{96,128},{128,160},{160,192},{192,224},{1,3... | collective-permute-start | bytes 1572872 | tf_op jit(solution)/shard_map/while/body/eval_jaxpr/ppermute | solution.py:25
  130.3 10.5 %collective-permute-start = (bf16[32,8192]{1,0:T(8,128)(2,1)S(1)}, bf16[32,8192]{1,0:T(8,128)(2,1)S(1)}, u32[]{:S(2)}, u32[]{:S(2)}) collective-permute-start(bf16[32,8192]{1,0:T(8,128)(2,1)S(1)} %fusion.73), channel_id=1, source_target_pairs={{0,32},{32,64},{64,96},{96,128},{128,160},{160,192},{192,224},{1,3... | collective-permute-start | bytes 1572872 | tf_op jit(solution)/shard_map/while/body/eval_jaxpr/ppermute | solution.py:25
  146.5 10.5 %collective-permute-start = (bf16[32,8192]{1,0:T(8,128)(2,1)S(1)}, bf16[32,8192]{1,0:T(8,128)(2,1)S(1)}, u32[]{:S(2)}, u32[]{:S(2)}) collective-permute-start(bf16[32,8192]{1,0:T(8,128)(2,1)S(1)} %fusion.73), channel_id=1, source_target_pairs={{0,32},{32,64},{64,96},{96,128},{128,160},{160,192},{192,224},{1,3... | collective-permute-start | bytes 1572872 | tf_op jit(solution)/shard_map/while/body/eval_jaxpr/ppermute | solution.py:25
  162.7 10.5 %collective-permute-start = (bf16[32,8192]{1,0:T(8,128)(2,1)S(1)}, bf16[32,8192]{1,0:T(8,128)(2,1)S(1)}, u32[]{:S(2)}, u32[]{:S(2)}) collective-permute-start(bf16[32,8192]{1,0:T(8,128)(2,1)S(1)} %fusion.73), channel_id=1, source_target_pairs={{0,32},{32,64},{64,96},{96,128},{128,160},{160,192},{192,224},{1,3... | collective-permute-start | bytes 1572872 | tf_op jit(solution)/shard_map/while/body/eval_jaxpr/ppermute | solution.py:25
  174.4 3.6 copy-start
  178.9 10.5 %collective-permute-start = (bf16[32,8192]{1,0:T(8,128)(2,1)S(1)}, bf16[32,8192]{1,0:T(8,128)(2,1)S(1)}, u32[]{:S(2)}, u32[]{:S(2)}) collective-permute-start(bf16[32,8192]{1,0:T(8,128)(2,1)S(1)} %fusion.73), channel_id=1, source_target_pairs={{0,32},{32,64},{64,96},{96,128},{128,160},{160,192},{192,224},{1,3... | collective-permute-start | bytes 1572872 | tf_op jit(solution)/shard_map/while/body/eval_jaxpr/ppermute | solution.py:25
  190.7 3.6 copy-start
  195.1 10.5 %collective-permute-start = (bf16[32,8192]{1,0:T(8,128)(2,1)S(1)}, bf16[32,8192]{1,0:T(8,128)(2,1)S(1)}, u32[]{:S(2)}, u32[]{:S(2)}) collective-permute-start(bf16[32,8192]{1,0:T(8,128)(2,1)S(1)} %fusion.73), channel_id=1, source_target_pairs={{0,32},{32,64},{64,96},{96,128},{128,160},{160,192},{192,224},{1,3... | collective-permute-start | bytes 1572872 | tf_op jit(solution)/shard_map/while/body/eval_jaxpr/ppermute | solution.py:25
  206.9 3.6 copy-start
  211.4 10.5 %collective-permute-start = (bf16[32,8192]{1,0:T(8,128)(2,1)S(1)}, bf16[32,8192]{1,0:T(8,128)(2,1)S(1)}, u32[]{:S(2)}, u32[]{:S(2)}) collective-permute-start(bf16[32,8192]{1,0:T(8,128)(2,1)S(1)} %fusion.73), channel_id=1, source_target_pairs={{0,32},{32,64},{64,96},{96,128},{128,160},{160,192},{192,224},{1,3... | collective-permute-start | bytes 1572872 | tf_op jit(solution)/shard_map/while/body/eval_jaxpr/ppermute | solution.py:25
  223.1 3.6 copy-start
  227.6 10.5 %collective-permute-start = (bf16[32,8192]{1,0:T(8,128)(2,1)S(1)}, bf16[32,8192]{1,0:T(8,128)(2,1)S(1)}, u32[]{:S(2)}, u32[]{:S(2)}) collective-permute-start(bf16[32,8192]{1,0:T(8,128)(2,1)S(1)} %fusion.73), channel_id=1, source_target_pairs={{0,32},{32,64},{64,96},{96,128},{128,160},{160,192},{192,224},{1,3... | collective-permute-start | bytes 1572872 | tf_op jit(solution)/shard_map/while/body/eval_jaxpr/ppermute | solution.py:25
  243.8 10.5 %collective-permute-start = (bf16[32,8192]{1,0:T(8,128)(2,1)S(1)}, bf16[32,8192]{1,0:T(8,128)(2,1)S(1)}, u32[]{:S(2)}, u32[]{:S(2)}) collective-permute-start(bf16[32,8192]{1,0:T(8,128)(2,1)S(1)} %fusion.73), channel_id=1, source_target_pairs={{0,32},{32,64},{64,96},{96,128},{128,160},{160,192},{192,224},{1,3... | collective-permute-start | bytes 1572872 | tf_op jit(solution)/shard_map/while/body/eval_jaxpr/ppermute | solution.py:25
  255.5 3.6 copy-start
  260.0 10.5 %collective-permute-start = (bf16[32,8192]{1,0:T(8,128)(2,1)S(1)}, bf16[32,8192]{1,0:T(8,128)(2,1)S(1)}, u32[]{:S(2)}, u32[]{:S(2)}) collective-permute-start(bf16[32,8192]{1,0:T(8,128)(2,1)S(1)} %fusion.73), channel_id=1, source_target_pairs={{0,32},{32,64},{64,96},{96,128},{128,160},{160,192},{192,224},{1,3... | collective-permute-start | bytes 1572872 | tf_op jit(solution)/shard_map/while/body/eval_jaxpr/ppermute | solution.py:25
  271.7 3.6 copy-start
  276.2 10.5 %collective-permute-start = (bf16[32,8192]{1,0:T(8,128)(2,1)S(1)}, bf16[32,8192]{1,0:T(8,128)(2,1)S(1)}, u32[]{:S(2)}, u32[]{:S(2)}) collective-permute-start(bf16[32,8192]{1,0:T(8,128)(2,1)S(1)} %fusion.73), channel_id=1, source_target_pairs={{0,32},{32,64},{64,96},{96,128},{128,160},{160,192},{192,224},{1,3... | collective-permute-start | bytes 1572872 | tf_op jit(solution)/shard_map/while/body/eval_jaxpr/ppermute | solution.py:25
  288.4 211.3 %copy-start.5 = (s32[4,2]{0,1:T(2,128)S(1)}, s32[4,2]{0,1:T(2,128)}, u32[]{:S(2)}) copy-start(s32[4,2]{0,1:T(2,128)} %param.17) | copy-start | bytes 100
  296.4 8.6 %collective-permute-start.1 = (bf16[32,8192]{1,0:T(8,128)(2,1)S(1)}, bf16[32,8192]{1,0:T(8,128)(2,1)S(1)}, u32[]{:S(2)}, u32[]{:S(2)}) collective-permute-start(bf16[32,8192]{1,0:T(8,128)(2,1)S(1)} %fusion.86), channel_id=1, source_target_pairs={{32,0},{64,32},{96,64},{128,96},{160,128},{192,160},{224,192},{33,... | collective-permute-start | bytes 1572872 | tf_op jit(solution)/shard_map/while/body/eval_jaxpr/ppermute | solution.py:25
  313.0 10.5 %collective-permute-start.1 = (bf16[32,8192]{1,0:T(8,128)(2,1)S(1)}, bf16[32,8192]{1,0:T(8,128)(2,1)S(1)}, u32[]{:S(2)}, u32[]{:S(2)}) collective-permute-start(bf16[32,8192]{1,0:T(8,128)(2,1)S(1)} %fusion.86), channel_id=1, source_target_pairs={{32,0},{64,32},{96,64},{128,96},{160,128},{192,160},{224,192},{33,... | collective-permute-start | bytes 1572872 | tf_op jit(solution)/shard_map/while/body/eval_jaxpr/ppermute | solution.py:25
  331.5 10.5 %collective-permute-start.1 = (bf16[32,8192]{1,0:T(8,128)(2,1)S(1)}, bf16[32,8192]{1,0:T(8,128)(2,1)S(1)}, u32[]{:S(2)}, u32[]{:S(2)}) collective-permute-start(bf16[32,8192]{1,0:T(8,128)(2,1)S(1)} %fusion.86), channel_id=1, source_target_pairs={{32,0},{64,32},{96,64},{128,96},{160,128},{192,160},{224,192},{33,... | collective-permute-start | bytes 1572872 | tf_op jit(solution)/shard_map/while/body/eval_jaxpr/ppermute | solution.py:25
  350.0 10.5 %collective-permute-start.1 = (bf16[32,8192]{1,0:T(8,128)(2,1)S(1)}, bf16[32,8192]{1,0:T(8,128)(2,1)S(1)}, u32[]{:S(2)}, u32[]{:S(2)}) collective-permute-start(bf16[32,8192]{1,0:T(8,128)(2,1)S(1)} %fusion.86), channel_id=1, source_target_pairs={{32,0},{64,32},{96,64},{128,96},{160,128},{192,160},{224,192},{33,... | collective-permute-start | bytes 1572872 | tf_op jit(solution)/shard_map/while/body/eval_jaxpr/ppermute | solution.py:25
  368.5 10.5 %collective-permute-start.1 = (bf16[32,8192]{1,0:T(8,128)(2,1)S(1)}, bf16[32,8192]{1,0:T(8,128)(2,1)S(1)}, u32[]{:S(2)}, u32[]{:S(2)}) collective-permute-start(bf16[32,8192]{1,0:T(8,128)(2,1)S(1)} %fusion.86), channel_id=1, source_target_pairs={{32,0},{64,32},{96,64},{128,96},{160,128},{192,160},{224,192},{33,... | collective-permute-start | bytes 1572872 | tf_op jit(solution)/shard_map/while/body/eval_jaxpr/ppermute | solution.py:25
  387.0 10.5 %collective-permute-start.1 = (bf16[32,8192]{1,0:T(8,128)(2,1)S(1)}, bf16[32,8192]{1,0:T(8,128)(2,1)S(1)}, u32[]{:S(2)}, u32[]{:S(2)}) collective-permute-start(bf16[32,8192]{1,0:T(8,128)(2,1)S(1)} %fusion.86), channel_id=1, source_target_pairs={{32,0},{64,32},{96,64},{128,96},{160,128},{192,160},{224,192},{33,... | collective-permute-start | bytes 1572872 | tf_op jit(solution)/shard_map/while/body/eval_jaxpr/ppermute | solution.py:25
  405.5 10.5 %collective-permute-start.1 = (bf16[32,8192]{1,0:T(8,128)(2,1)S(1)}, bf16[32,8192]{1,0:T(8,128)(2,1)S(1)}, u32[]{:S(2)}, u32[]{:S(2)}) collective-permute-start(bf16[32,8192]{1,0:T(8,128)(2,1)S(1)} %fusion.86), channel_id=1, source_target_pairs={{32,0},{64,32},{96,64},{128,96},{160,128},{192,160},{224,192},{33,... | collective-permute-start | bytes 1572872 | tf_op jit(solution)/shard_map/while/body/eval_jaxpr/ppermute | solution.py:25
  424.0 10.5 %collective-permute-start.1 = (bf16[32,8192]{1,0:T(8,128)(2,1)S(1)}, bf16[32,8192]{1,0:T(8,128)(2,1)S(1)}, u32[]{:S(2)}, u32[]{:S(2)}) collective-permute-start(bf16[32,8192]{1,0:T(8,128)(2,1)S(1)} %fusion.86), channel_id=1, source_target_pairs={{32,0},{64,32},{96,64},{128,96},{160,128},{192,160},{224,192},{33,... | collective-permute-start | bytes 1572872 | tf_op jit(solution)/shard_map/while/body/eval_jaxpr/ppermute | solution.py:25
  442.5 10.4 %collective-permute-start.1 = (bf16[32,8192]{1,0:T(8,128)(2,1)S(1)}, bf16[32,8192]{1,0:T(8,128)(2,1)S(1)}, u32[]{:S(2)}, u32[]{:S(2)}) collective-permute-start(bf16[32,8192]{1,0:T(8,128)(2,1)S(1)} %fusion.86), channel_id=1, source_target_pairs={{32,0},{64,32},{96,64},{128,96},{160,128},{192,160},{224,192},{33,... | collective-permute-start | bytes 1572872 | tf_op jit(solution)/shard_map/while/body/eval_jaxpr/ppermute | solution.py:25
  461.0 10.5 %collective-permute-start.1 = (bf16[32,8192]{1,0:T(8,128)(2,1)S(1)}, bf16[32,8192]{1,0:T(8,128)(2,1)S(1)}, u32[]{:S(2)}, u32[]{:S(2)}) collective-permute-start(bf16[32,8192]{1,0:T(8,128)(2,1)S(1)} %fusion.86), channel_id=1, source_target_pairs={{32,0},{64,32},{96,64},{128,96},{160,128},{192,160},{224,192},{33,... | collective-permute-start | bytes 1572872 | tf_op jit(solution)/shard_map/while/body/eval_jaxpr/ppermute | solution.py:25
  479.5 10.5 %collective-permute-start.1 = (bf16[32,8192]{1,0:T(8,128)(2,1)S(1)}, bf16[32,8192]{1,0:T(8,128)(2,1)S(1)}, u32[]{:S(2)}, u32[]{:S(2)}) collective-permute-start(bf16[32,8192]{1,0:T(8,128)(2,1)S(1)} %fusion.86), channel_id=1, source_target_pairs={{32,0},{64,32},{96,64},{128,96},{160,128},{192,160},{224,192},{33,... | collective-permute-start | bytes 1572872 | tf_op jit(solution)/shard_map/while/body/eval_jaxpr/ppermute | solution.py:25
  505.6 80.7 %reduce-scatter.5.cloned.1.call-start = ((), (), s32[]{:S(2)}) async-start(), calls=%async_computation.5 | async-start | bytes 655360 | tf_op jit(solution)/shard_map/reduce_scatter | solution.py:40
  (29 other events, 90.9 us)
Sparse Core Ops, SparseCore 0:
  10.4 85.8 all-gather.1
  505.7 55.2 reduce-scatter.2
  563.6 22.7 reduce-scatter.4
where the time goes:
time: 599 us; the launch traced here: 595 us
  waiting for transfers between devices  279 us (47%)
  other arithmetic  87.2 us (15%)
  local copies, waits for them, and re-layouts  74 us (12%)
  starting transfers between devices  61.3 us (10%)
  matrix products  54.8 us (9%)
  loops' own time  15.8 us (3%)
  between operations  13.9 us (2%)
  blocking collectives  9.53 us (2%)
    ppermute x22, waiting for transfers between devices, from_behind(): return lax.ppermute(block, axis, route)  112 us
    all_gather x1, waiting for transfers between devices, gather_turned(): result, at, done = (lax.all_gather(both, axis, axis=0, tiled=True), 0, [])  85.9 us
    reduce_scatter x2, waiting for transfers between devices, summed_rows(): running = lax.psum_scatter(running, axis, scatter_dimension=0, tiled=True)  80.7 us
    ppermute x22, starting transfers between devices, from_behind(): return lax.ppermute(block, axis, route)  61.2 us
    dynamic_update_slice x33, other arithmetic, place(): lax.dynamic_update_index_in_dim(store, jnp.where(active, value, old), ind...  58.9 us
    dot_general x66, matrix products, contract_last(): lax.dot_general(left, right, (((1,), (1,)), ((), ())), preferred_element_...  41.6 us
    dynamic_slice x55, local copies, waits for them, and re-layouts, place(): old = lax.dynamic_index_in_dim(store, index, 0, keepdims=False)  37.5 us
    reduce_sum x22, other arithmetic, normalize(): scale = lax.rsqrt(jnp.mean(stream * stream, -1, keepdims=True) + 1e-05)  16.4 us
  transfers between devices with their start and end apart: 25, of which 25 were waited for; matrix products, arithmetic and copies ran while one was open for 9% of the time, Pallas kernels for 0%

commit v1 on v0

--- a/solution.py
+++ b/solution.py
@@ -11,7 +11,13 @@
 def gather_turned(arrays, axis, dims):
     turned = [jnp.moveaxis(a, dim, 0) for a, dim in zip(arrays, dims)]
     both = jnp.concatenate([t.reshape(len(t), -1) for t in turned], axis=1)
-    result, at, done = (lax.all_gather(both, axis, axis=0, tiled=True), 0, [])
+    result, at, done = (
+        jnp.concatenate(
+            lax.all_to_all(jnp.stack([both] * lax.axis_size(axis)), axis, 0, 0), axis=0
+        ),
+        0,
+        [],
+    )
     for t, dim in zip(turned, dims):
         section = result[:, at : at + t[0].size].reshape(-1, *t.shape[1:])
         done.append(jnp.moveaxis(section, 0, dim))

time: 599 us -> 625 us (1.043)
  waiting for transfers between devices: 279 us -> 295 us
  starting transfers between devices: 61.3 us -> 72.8 us
    all_to_all x0 -> x1, waiting for transfers between devices: none -> 96.9 us  [gather_turned(): lax.all_to_all(jnp.stack([both] * lax.axis_size(axis)), axis, 0, 0)]
    all_gather x1 -> x0, waiting for transfers between devices: 85.9 us -> none  [gather_turned(): result, at, done = (lax.all_gather(both, axis, axis=0, tiled=True), 0, [])]
    all_to_all x0 -> x1, starting transfers between devices: none -> 11.6 us  [gather_turned(): lax.all_to_all(jnp.stack([both] * lax.axis_size(axis)), axis, 0, 0)]
    eq x11, local copies, waits for them, and re-layouts: 7.78 us -> 0.06 us  [ghost(): same = owners[:, None] == owners[None, :]]
    ppermute x22, waiting for transfers between devices: 112 us -> 120 us  [from_behind(): return lax.ppermute(block, axis, route)]
  transfers between devices with their start and end apart: 25 -> 25, of which waited for: 25 -> 25; matrix products, arithmetic and copies ran while one was open for 9% -> 8% of each run, Pallas kernels for 0% -> 0%
where the time goes in v1:
time: 625 us; the launch traced here: 622 us
  waiting for transfers between devices  295 us (47%)
  other arithmetic  84.9 us (14%)
  local copies, waits for them, and re-layouts  75 us (12%)
  starting transfers between devices  72.8 us (12%)
  matrix products  55.1 us (9%)
  loops' own time  15.3 us (2%)
  between operations  14.2 us (2%)
  blocking collectives  9.69 us (2%)
    ppermute x22, waiting for transfers between devices, from_behind(): return lax.ppermute(block, axis, route)  120 us
    all_to_all x1, waiting for transfers between devices, gather_turned(): lax.all_to_all(jnp.stack([both] * lax.axis_size(axis)), axis, 0, 0)  96.9 us
    reduce_scatter x2, waiting for transfers between devices, summed_rows(): running = lax.psum_scatter(running, axis, scatter_dimension=0, tiled=True)  78.4 us
    ppermute x22, starting transfers between devices, from_behind(): return lax.ppermute(block, axis, route)  61.2 us
    dynamic_update_slice x33, other arithmetic, place(): lax.dynamic_update_index_in_dim(store, jnp.where(active, value, old), ind...  58.8 us
    dot_general x66, matrix products, contract_last(): lax.dot_general(left, right, (((1,), (1,)), ((), ())), preferred_element_...  41.9 us
    dynamic_slice x55, local copies, waits for them, and re-layouts, place(): old = lax.dynamic_index_in_dim(store, index, 0, keepdims=False)  37.5 us
    reduce_sum x22, other arithmetic, normalize(): scale = lax.rsqrt(jnp.mean(stream * stream, -1, keepdims=True) + 1e-05)  16.4 us
  transfers between devices with their start and end apart: 25, of which 25 were waited for; matrix products, arithmetic and copies ran while one was open for 8% of the time, Pallas kernels for 0%

profile of v1, /device:TPU:8, one launch (start us, length us, event | category | flops | bytes accessed | tf_op | source)
XLA Modules:
  0.0 621.9 jit_solution(3064682507843160051)
XLA Ops:
  11.3 11.6 %all-to-all-start = ((bf16[32,256,257]{1,2,0:T(8,128)(2,1)}), bf16[32,256,257]{1,2,0:T(8,128)(2,1)}, u32[]{:S(2)}, u32[]{:S(2)}) async-start(bf16[32,256,257]{1,2,0:T(8,128)(2,1)} %stack.2), calls=%async_computation | async-start | bytes 8650752 | tf_op jit(solution)/shard_map/all_to_all | solution.py:16
  22.9 96.9 %all-to-all-done = bf16[32,256,257]{1,2,0:T(8,128)(2,1)} async-done(((bf16[32,256,257]{1,2,0:T(8,128)(2,1)}), bf16[32,256,257]{1,2,0:T(8,128)(2,1)}, u32[]{:S(2)}, u32[]{:S(2)}) %all-to-all-start) | async-done | bytes 4210720 | tf_op jit(solution)/shard_map/all_to_all | solution.py:16
  123.5 5.1 copy.26
  130.3 4.1 copy.21
  137.5 177.8 %while.35 = (s32[]{:T(128)}, bf16[32,8192]{1,0:T(8,128)(2,1)S(1)}, bf16[4,32,8192]{2,1,0:T(8,128)(2,1)}, bf16[4,32,8192]{2,1,0:T(8,128)(2,1)}, bf16[4,32,128]{2,...) while((s32[]{:T(128)}, bf16[32,8192]{1,0:T(8,128)(2,1)S(1)}, ...), condition=%wide.region_2.3_spmd, body=%wide.region_0.2_spmd.sunk | while | flops 138682400 | bytes 23185208 | solution.py:125
  147.2 6.4 %collective-permute-done = bf16[32,8192]{1,0:T(8,128)(2,1)S(1)} collective-permute-done((bf16[32,8192]{1,0:T(8,128)(2,1)S(1)}, bf16[32,8192]{1,0:T(8,128)(2,1)S(1)}, u32[]{:S(2)}, u32[]{:S(2)}) %collective-permute-start) | collective-permute-done | bytes 524320 | tf_op jit(solution)/shard_map/while/body/eval_jaxpr/ppermute | solution.py:31
  163.4 6.4 %collective-permute-done = bf16[32,8192]{1,0:T(8,128)(2,1)S(1)} collective-permute-done((bf16[32,8192]{1,0:T(8,128)(2,1)S(1)}, bf16[32,8192]{1,0:T(8,128)(2,1)S(1)}, u32[]{:S(2)}, u32[]{:S(2)}) %collective-permute-start) | collective-permute-done | bytes 524320 | tf_op jit(solution)/shard_map/while/body/eval_jaxpr/ppermute | solution.py:31
  179.6 6.4 %collective-permute-done = bf16[32,8192]{1,0:T(8,128)(2,1)S(1)} collective-permute-done((bf16[32,8192]{1,0:T(8,128)(2,1)S(1)}, bf16[32,8192]{1,0:T(8,128)(2,1)S(1)}, u32[]{:S(2)}, u32[]{:S(2)}) %collective-permute-start) | collective-permute-done | bytes 524320 | tf_op jit(solution)/shard_map/while/body/eval_jaxpr/ppermute | solution.py:31
  195.7 6.4 %collective-permute-done = bf16[32,8192]{1,0:T(8,128)(2,1)S(1)} collective-permute-done((bf16[32,8192]{1,0:T(8,128)(2,1)S(1)}, bf16[32,8192]{1,0:T(8,128)(2,1)S(1)}, u32[]{:S(2)}, u32[]{:S(2)}) %collective-permute-start) | collective-permute-done | bytes 524320 | tf_op jit(solution)/shard_map/while/body/eval_jaxpr/ppermute | solution.py:31
  211.9 6.4 %collective-permute-done = bf16[32,8192]{1,0:T(8,128)(2,1)S(1)} collective-permute-done((bf16[32,8192]{1,0:T(8,128)(2,1)S(1)}, bf16[32,8192]{1,0:T(8,128)(2,1)S(1)}, u32[]{:S(2)}, u32[]{:S(2)}) %collective-permute-start) | collective-permute-done | bytes 524320 | tf_op jit(solution)/shard_map/while/body/eval_jaxpr/ppermute | solution.py:31
  228.1 6.4 %collective-permute-done = bf16[32,8192]{1,0:T(8,128)(2,1)S(1)} collective-permute-done((bf16[32,8192]{1,0:T(8,128)(2,1)S(1)}, bf16[32,8192]{1,0:T(8,128)(2,1)S(1)}, u32[]{:S(2)}, u32[]{:S(2)}) %collective-permute-start) | collective-permute-done | bytes 524320 | tf_op jit(solution)/shard_map/while/body/eval_jaxpr/ppermute | solution.py:31
  244.2 6.4 %collective-permute-done = bf16[32,8192]{1,0:T(8,128)(2,1)S(1)} collective-permute-done((bf16[32,8192]{1,0:T(8,128)(2,1)S(1)}, bf16[32,8192]{1,0:T(8,128)(2,1)S(1)}, u32[]{:S(2)}, u32[]{:S(2)}) %collective-permute-start) | collective-permute-done | bytes 524320 | tf_op jit(solution)/shard_map/while/body/eval_jaxpr/ppermute | solution.py:31
  260.4 6.4 %collective-permute-done = bf16[32,8192]{1,0:T(8,128)(2,1)S(1)} collective-permute-done((bf16[32,8192]{1,0:T(8,128)(2,1)S(1)}, bf16[32,8192]{1,0:T(8,128)(2,1)S(1)}, u32[]{:S(2)}, u32[]{:S(2)}) %collective-permute-start) | collective-permute-done | bytes 524320 | tf_op jit(solution)/shard_map/while/body/eval_jaxpr/ppermute | solution.py:31
  276.6 6.4 %collective-permute-done = bf16[32,8192]{1,0:T(8,128)(2,1)S(1)} collective-permute-done((bf16[32,8192]{1,0:T(8,128)(2,1)S(1)}, bf16[32,8192]{1,0:T(8,128)(2,1)S(1)}, u32[]{:S(2)}, u32[]{:S(2)}) %collective-permute-start) | collective-permute-done | bytes 524320 | tf_op jit(solution)/shard_map/while/body/eval_jaxpr/ppermute | solution.py:31
  292.7 6.4 %collective-permute-done = bf16[32,8192]{1,0:T(8,128)(2,1)S(1)} collective-permute-done((bf16[32,8192]{1,0:T(8,128)(2,1)S(1)}, bf16[32,8192]{1,0:T(8,128)(2,1)S(1)}, u32[]{:S(2)}, u32[]{:S(2)}) %collective-permute-start) | collective-permute-done | bytes 524320 | tf_op jit(solution)/shard_map/while/body/eval_jaxpr/ppermute | solution.py:31
  308.9 6.4 %collective-permute-done = bf16[32,8192]{1,0:T(8,128)(2,1)S(1)} collective-permute-done((bf16[32,8192]{1,0:T(8,128)(2,1)S(1)}, bf16[32,8192]{1,0:T(8,128)(2,1)S(1)}, u32[]{:S(2)}, u32[]{:S(2)}) %collective-permute-start) | collective-permute-done | bytes 524320 | tf_op jit(solution)/shard_map/while/body/eval_jaxpr/ppermute | solution.py:31
  316.9 201.5 %while.36 = (s32[]{:T(128)}, bf16[32,8192]{1,0:T(8,128)(2,1)S(1)}, bf16[4,32,128]{2,1,0:T(8,128)(2,1)S(1)}, bf16[4,32,8192]{2,1,0:T(8,128)(2,1)}, f32[4,2]{1,0:T...) while((s32[]{:T(128)}, bf16[32,8192]{1,0:T(8,128)(2,1)S(1)}, ...), condition=%wide.region_8.9_spmd, body=%wide.region_3.8_spmd.sunk | while | flops 173029504 | bytes 33156040 | solution.py:160
  329.1 4.5 collective-permute-done.1
  347.6 4.5 collective-permute-done.1
  366.1 4.5 collective-permute-done.1
  384.6 4.5 collective-permute-done.1
  403.1 4.5 collective-permute-done.1
  421.6 4.5 collective-permute-done.1
  440.1 4.4 collective-permute-done.1
  452.5 3.9 collective-permute-start.1
  458.6 4.5 collective-permute-done.1
  477.1 4.4 collective-permute-done.1
  495.6 4.4 collective-permute-done.1
  514.1 4.4 collective-permute-done.1
  518.6 9.7 %all_to_all.10 = f32[8,4,2]{1,2,0:T(2,128)S(1)} all-to-all(f32[8,4,2]{1,2,0:T(2,128)S(1)} %broadcast_in_dim.47), channel_id=1, replica_groups=mesh['section'=8,'dp_0'=8,'dp_1'=4] {'section'}, dimensions={0} | all-to-all | bytes 512 | tf_op jit(solution)/shard_map/all_to_all | solution.py:36
  534.3 53.0 %reduce-scatter.3.cloned.1.call-done = bf16[1024,256]{0,1:T(8,128)(2,1)} async-done(((bf16[8192,256]{0,1:T(8,128)(2,1)}), bf16[1024,256]{0,1:T(8,128)(2,1)}) %reduce-scatter.3.cloned.1.call-update) | async-done | bytes 524304 | tf_op jit(solution)/shard_map/reduce_scatter | solution.py:46
  587.4 25.3 %reduce-scatter.5.cloned.1.call-done = bf16[256,256]{0,1:T(8,128)(2,1)} async-done(((bf16[1024,256]{0,1:T(8,128)(2,1)}), bf16[256,256]{0,1:T(8,128)(2,1)}) %reduce-scatter.5.cloned.1.call-update) | async-done | bytes 131088 | tf_op jit(solution)/shard_map/reduce_scatter | solution.py:46
  (438 shorter events, 263.3 us)
Async XLA Ops:
  11.3 11.6 %copy-start.5 = (s32[4,32]{1,0:T(4,128)S(1)}, s32[4,32]{1,0:T(4,128)}, u32[]{:S(2)}) copy-start(s32[4,32]{1,0:T(4,128)} %param.16) | copy-start | bytes 1540
  11.3 108.6 %all-to-all-start = ((bf16[32,256,257]{1,2,0:T(8,128)(2,1)}), bf16[32,256,257]{1,2,0:T(8,128)(2,1)}, u32[]{:S(2)}, u32[]{:S(2)}) async-start(bf16[32,256,257]{1,2,0:T(8,128)(2,1)} %stack.2), calls=%async_computation | async-start | bytes 8650752 | tf_op jit(solution)/shard_map/all_to_all | solution.py:16
  22.8 564.5 %reduce-scatter.3.cloned.1.call-start = ((), (), s32[]{:S(2)}) async-start(), calls=%async_computation.4 | async-start | bytes 4718592 | tf_op jit(solution)/shard_map/reduce_scatter | solution.py:46
  143.2 10.5 %collective-permute-start = (bf16[32,8192]{1,0:T(8,128)(2,1)S(1)}, bf16[32,8192]{1,0:T(8,128)(2,1)S(1)}, u32[]{:S(2)}, u32[]{:S(2)}) collective-permute-start(bf16[32,8192]{1,0:T(8,128)(2,1)S(1)} %fusion.73), channel_id=1, source_target_pairs={{0,32},{32,64},{64,96},{96,128},{128,160},{160,192},{192,224},{1,3... | collective-permute-start | bytes 1572872 | tf_op jit(solution)/shard_map/while/body/eval_jaxpr/ppermute | solution.py:31
  159.3 10.5 %collective-permute-start = (bf16[32,8192]{1,0:T(8,128)(2,1)S(1)}, bf16[32,8192]{1,0:T(8,128)(2,1)S(1)}, u32[]{:S(2)}, u32[]{:S(2)}) collective-permute-start(bf16[32,8192]{1,0:T(8,128)(2,1)S(1)} %fusion.73), channel_id=1, source_target_pairs={{0,32},{32,64},{64,96},{96,128},{128,160},{160,192},{192,224},{1,3... | collective-permute-start | bytes 1572872 | tf_op jit(solution)/shard_map/while/body/eval_jaxpr/ppermute | solution.py:31
  175.5 10.5 %collective-permute-start = (bf16[32,8192]{1,0:T(8,128)(2,1)S(1)}, bf16[32,8192]{1,0:T(8,128)(2,1)S(1)}, u32[]{:S(2)}, u32[]{:S(2)}) collective-permute-start(bf16[32,8192]{1,0:T(8,128)(2,1)S(1)} %fusion.73), channel_id=1, source_target_pairs={{0,32},{32,64},{64,96},{96,128},{128,160},{160,192},{192,224},{1,3... | collective-permute-start | bytes 1572872 | tf_op jit(solution)/shard_map/while/body/eval_jaxpr/ppermute | solution.py:31
  191.7 10.5 %collective-permute-start = (bf16[32,8192]{1,0:T(8,128)(2,1)S(1)}, bf16[32,8192]{1,0:T(8,128)(2,1)S(1)}, u32[]{:S(2)}, u32[]{:S(2)}) collective-permute-start(bf16[32,8192]{1,0:T(8,128)(2,1)S(1)} %fusion.73), channel_id=1, source_target_pairs={{0,32},{32,64},{64,96},{96,128},{128,160},{160,192},{192,224},{1,3... | collective-permute-start | bytes 1572872 | tf_op jit(solution)/shard_map/while/body/eval_jaxpr/ppermute | solution.py:31
  207.8 10.5 %collective-permute-start = (bf16[32,8192]{1,0:T(8,128)(2,1)S(1)}, bf16[32,8192]{1,0:T(8,128)(2,1)S(1)}, u32[]{:S(2)}, u32[]{:S(2)}) collective-permute-start(bf16[32,8192]{1,0:T(8,128)(2,1)S(1)} %fusion.73), channel_id=1, source_target_pairs={{0,32},{32,64},{64,96},{96,128},{128,160},{160,192},{192,224},{1,3... | collective-permute-start | bytes 1572872 | tf_op jit(solution)/shard_map/while/body/eval_jaxpr/ppermute | solution.py:31
  224.0 10.5 %collective-permute-start = (bf16[32,8192]{1,0:T(8,128)(2,1)S(1)}, bf16[32,8192]{1,0:T(8,128)(2,1)S(1)}, u32[]{:S(2)}, u32[]{:S(2)}) collective-permute-start(bf16[32,8192]{1,0:T(8,128)(2,1)S(1)} %fusion.73), channel_id=1, source_target_pairs={{0,32},{32,64},{64,96},{96,128},{128,160},{160,192},{192,224},{1,3... | collective-permute-start | bytes 1572872 | tf_op jit(solution)/shard_map/while/body/eval_jaxpr/ppermute | solution.py:31
  235.7 3.6 copy-start
  240.1 10.5 %collective-permute-start = (bf16[32,8192]{1,0:T(8,128)(2,1)S(1)}, bf16[32,8192]{1,0:T(8,128)(2,1)S(1)}, u32[]{:S(2)}, u32[]{:S(2)}) collective-permute-start(bf16[32,8192]{1,0:T(8,128)(2,1)S(1)} %fusion.73), channel_id=1, source_target_pairs={{0,32},{32,64},{64,96},{96,128},{128,160},{160,192},{192,224},{1,3... | collective-permute-start | bytes 1572872 | tf_op jit(solution)/shard_map/while/body/eval_jaxpr/ppermute | solution.py:31
  251.8 3.6 copy-start
  256.3 10.5 %collective-permute-start = (bf16[32,8192]{1,0:T(8,128)(2,1)S(1)}, bf16[32,8192]{1,0:T(8,128)(2,1)S(1)}, u32[]{:S(2)}, u32[]{:S(2)}) collective-permute-start(bf16[32,8192]{1,0:T(8,128)(2,1)S(1)} %fusion.73), channel_id=1, source_target_pairs={{0,32},{32,64},{64,96},{96,128},{128,160},{160,192},{192,224},{1,3... | collective-permute-start | bytes 1572872 | tf_op jit(solution)/shard_map/while/body/eval_jaxpr/ppermute | solution.py:31
  268.0 3.6 copy-start
  272.5 10.5 %collective-permute-start = (bf16[32,8192]{1,0:T(8,128)(2,1)S(1)}, bf16[32,8192]{1,0:T(8,128)(2,1)S(1)}, u32[]{:S(2)}, u32[]{:S(2)}) collective-permute-start(bf16[32,8192]{1,0:T(8,128)(2,1)S(1)} %fusion.73), channel_id=1, source_target_pairs={{0,32},{32,64},{64,96},{96,128},{128,160},{160,192},{192,224},{1,3... | collective-permute-start | bytes 1572872 | tf_op jit(solution)/shard_map/while/body/eval_jaxpr/ppermute | solution.py:31
  284.2 3.6 copy-start
  288.6 10.5 %collective-permute-start = (bf16[32,8192]{1,0:T(8,128)(2,1)S(1)}, bf16[32,8192]{1,0:T(8,128)(2,1)S(1)}, u32[]{:S(2)}, u32[]{:S(2)}) collective-permute-start(bf16[32,8192]{1,0:T(8,128)(2,1)S(1)} %fusion.73), channel_id=1, source_target_pairs={{0,32},{32,64},{64,96},{96,128},{128,160},{160,192},{192,224},{1,3... | collective-permute-start | bytes 1572872 | tf_op jit(solution)/shard_map/while/body/eval_jaxpr/ppermute | solution.py:31
  300.3 3.6 copy-start
  304.8 10.5 %collective-permute-start = (bf16[32,8192]{1,0:T(8,128)(2,1)S(1)}, bf16[32,8192]{1,0:T(8,128)(2,1)S(1)}, u32[]{:S(2)}, u32[]{:S(2)}) collective-permute-start(bf16[32,8192]{1,0:T(8,128)(2,1)S(1)} %fusion.73), channel_id=1, source_target_pairs={{0,32},{32,64},{64,96},{96,128},{128,160},{160,192},{192,224},{1,3... | collective-permute-start | bytes 1572872 | tf_op jit(solution)/shard_map/while/body/eval_jaxpr/ppermute | solution.py:31
  316.9 211.4 %copy-start.6 = (s32[4,2]{0,1:T(2,128)S(1)}, s32[4,2]{0,1:T(2,128)}, u32[]{:S(2)}) copy-start(s32[4,2]{0,1:T(2,128)} %param.17) | copy-start | bytes 100
  325.0 8.6 %collective-permute-start.1 = (bf16[32,8192]{1,0:T(8,128)(2,1)S(1)}, bf16[32,8192]{1,0:T(8,128)(2,1)S(1)}, u32[]{:S(2)}, u32[]{:S(2)}) collective-permute-start(bf16[32,8192]{1,0:T(8,128)(2,1)S(1)} %fusion.86), channel_id=1, source_target_pairs={{32,0},{64,32},{96,64},{128,96},{160,128},{192,160},{224,192},{33,... | collective-permute-start | bytes 1572872 | tf_op jit(solution)/shard_map/while/body/eval_jaxpr/ppermute | solution.py:31
  341.6 10.5 %collective-permute-start.1 = (bf16[32,8192]{1,0:T(8,128)(2,1)S(1)}, bf16[32,8192]{1,0:T(8,128)(2,1)S(1)}, u32[]{:S(2)}, u32[]{:S(2)}) collective-permute-start(bf16[32,8192]{1,0:T(8,128)(2,1)S(1)} %fusion.86), channel_id=1, source_target_pairs={{32,0},{64,32},{96,64},{128,96},{160,128},{192,160},{224,192},{33,... | collective-permute-start | bytes 1572872 | tf_op jit(solution)/shard_map/while/body/eval_jaxpr/ppermute | solution.py:31
  360.1 10.5 %collective-permute-start.1 = (bf16[32,8192]{1,0:T(8,128)(2,1)S(1)}, bf16[32,8192]{1,0:T(8,128)(2,1)S(1)}, u32[]{:S(2)}, u32[]{:S(2)}) collective-permute-start(bf16[32,8192]{1,0:T(8,128)(2,1)S(1)} %fusion.86), channel_id=1, source_target_pairs={{32,0},{64,32},{96,64},{128,96},{160,128},{192,160},{224,192},{33,... | collective-permute-start | bytes 1572872 | tf_op jit(solution)/shard_map/while/body/eval_jaxpr/ppermute | solution.py:31
  378.5 10.5 %collective-permute-start.1 = (bf16[32,8192]{1,0:T(8,128)(2,1)S(1)}, bf16[32,8192]{1,0:T(8,128)(2,1)S(1)}, u32[]{:S(2)}, u32[]{:S(2)}) collective-permute-start(bf16[32,8192]{1,0:T(8,128)(2,1)S(1)} %fusion.86), channel_id=1, source_target_pairs={{32,0},{64,32},{96,64},{128,96},{160,128},{192,160},{224,192},{33,... | collective-permute-start | bytes 1572872 | tf_op jit(solution)/shard_map/while/body/eval_jaxpr/ppermute | solution.py:31
  397.0 10.5 %collective-permute-start.1 = (bf16[32,8192]{1,0:T(8,128)(2,1)S(1)}, bf16[32,8192]{1,0:T(8,128)(2,1)S(1)}, u32[]{:S(2)}, u32[]{:S(2)}) collective-permute-start(bf16[32,8192]{1,0:T(8,128)(2,1)S(1)} %fusion.86), channel_id=1, source_target_pairs={{32,0},{64,32},{96,64},{128,96},{160,128},{192,160},{224,192},{33,... | collective-permute-start | bytes 1572872 | tf_op jit(solution)/shard_map/while/body/eval_jaxpr/ppermute | solution.py:31
  415.5 10.5 %collective-permute-start.1 = (bf16[32,8192]{1,0:T(8,128)(2,1)S(1)}, bf16[32,8192]{1,0:T(8,128)(2,1)S(1)}, u32[]{:S(2)}, u32[]{:S(2)}) collective-permute-start(bf16[32,8192]{1,0:T(8,128)(2,1)S(1)} %fusion.86), channel_id=1, source_target_pairs={{32,0},{64,32},{96,64},{128,96},{160,128},{192,160},{224,192},{33,... | collective-permute-start | bytes 1572872 | tf_op jit(solution)/shard_map/while/body/eval_jaxpr/ppermute | solution.py:31
  434.0 10.5 %collective-permute-start.1 = (bf16[32,8192]{1,0:T(8,128)(2,1)S(1)}, bf16[32,8192]{1,0:T(8,128)(2,1)S(1)}, u32[]{:S(2)}, u32[]{:S(2)}) collective-permute-start(bf16[32,8192]{1,0:T(8,128)(2,1)S(1)} %fusion.86), channel_id=1, source_target_pairs={{32,0},{64,32},{96,64},{128,96},{160,128},{192,160},{224,192},{33,... | collective-permute-start | bytes 1572872 | tf_op jit(solution)/shard_map/while/body/eval_jaxpr/ppermute | solution.py:31
  452.5 10.5 %collective-permute-start.1 = (bf16[32,8192]{1,0:T(8,128)(2,1)S(1)}, bf16[32,8192]{1,0:T(8,128)(2,1)S(1)}, u32[]{:S(2)}, u32[]{:S(2)}) collective-permute-start(bf16[32,8192]{1,0:T(8,128)(2,1)S(1)} %fusion.86), channel_id=1, source_target_pairs={{32,0},{64,32},{96,64},{128,96},{160,128},{192,160},{224,192},{33,... | collective-permute-start | bytes 1572872 | tf_op jit(solution)/shard_map/while/body/eval_jaxpr/ppermute | solution.py:31
  471.0 10.5 %collective-permute-start.1 = (bf16[32,8192]{1,0:T(8,128)(2,1)S(1)}, bf16[32,8192]{1,0:T(8,128)(2,1)S(1)}, u32[]{:S(2)}, u32[]{:S(2)}) collective-permute-start(bf16[32,8192]{1,0:T(8,128)(2,1)S(1)} %fusion.86), channel_id=1, source_target_pairs={{32,0},{64,32},{96,64},{128,96},{160,128},{192,160},{224,192},{33,... | collective-permute-start | bytes 1572872 | tf_op jit(solution)/shard_map/while/body/eval_jaxpr/ppermute | solution.py:31
  489.5 10.5 %collective-permute-start.1 = (bf16[32,8192]{1,0:T(8,128)(2,1)S(1)}, bf16[32,8192]{1,0:T(8,128)(2,1)S(1)}, u32[]{:S(2)}, u32[]{:S(2)}) collective-permute-start(bf16[32,8192]{1,0:T(8,128)(2,1)S(1)} %fusion.86), channel_id=1, source_target_pairs={{32,0},{64,32},{96,64},{128,96},{160,128},{192,160},{224,192},{33,... | collective-permute-start | bytes 1572872 | tf_op jit(solution)/shard_map/while/body/eval_jaxpr/ppermute | solution.py:31
  508.0 10.5 %collective-permute-start.1 = (bf16[32,8192]{1,0:T(8,128)(2,1)S(1)}, bf16[32,8192]{1,0:T(8,128)(2,1)S(1)}, u32[]{:S(2)}, u32[]{:S(2)}) collective-permute-start(bf16[32,8192]{1,0:T(8,128)(2,1)S(1)} %fusion.86), channel_id=1, source_target_pairs={{32,0},{64,32},{96,64},{128,96},{160,128},{192,160},{224,192},{33,... | collective-permute-start | bytes 1572872 | tf_op jit(solution)/shard_map/while/body/eval_jaxpr/ppermute | solution.py:31
  534.3 78.4 %reduce-scatter.5.cloned.1.call-start = ((), (), s32[]{:S(2)}) async-start(), calls=%async_computation.5 | async-start | bytes 655360 | tf_op jit(solution)/shard_map/reduce_scatter | solution.py:46
  (30 other events, 94.4 us)
Sparse Core Ops, SparseCore 0:
  534.4 52.9 reduce-scatter.2
  589.9 22.7 reduce-scatter.4
